TPU v7x, 128 devices: a whole 4x4x4 slice. The times are simulated.
128 devices in a mesh: cell: 8 (over x, z_lo), rays: 16 (over y, z_hi, core).
Axes of the slice: x: 4, y: 4, z: 4 (z_hi: 2, z_lo: 2; z = z_hi * 2 + z_lo), core: 2. Of those that a mesh axis runs over, the one named last changes fastest.
Arguments:
- encodings: float32 [4096, 128, 256], P('rays', 'cell'), may hold values from -6 to 6
- spacing: float32 [4096, 128], P('rays', 'cell'), may hold values from 0.01 to 0.06
- counts: int32 [4096, 8], P('rays', 'cell'), may hold values from 1 to 16
- cell_weights: float32 [8, 4, 256, 256], P('cell'), may hold values from -0.375 to 0.375
- density_head: float32 [8, 256], P('cell'), may hold values from -0.75 to 0.75
- decoder_in: float32 [256, 256], replicated, may hold values from -0.75 to 0.75
- decoder_out: float32 [256, 3], replicated, may hold values from -0.375 to 0.375
- color_grad: float32 [4096, 3], P('rays'), may hold values from -0.75 to 0.75
Outputs:
- layer_grads: float32 [8, 4, 256, 256], P('cell')
- head_grads: float32 [8, 256], P('cell')
- decoder_in_grad: float32 [256, 256], replicated
- decoder_out_grad: float32 [256, 3], replicated
- sample_grad: float32 [4096, 128, 256], P('rays', 'cell')
Inputs may be any that keep to these rules, and one draw needn't show every extreme that they name: `counts`: live samples of a ray in a cell occupy the first slots of that cell.
All inputs are finite; a program needn't handle non-finite values.
Results may differ from a plain program's by a relative error of at most 0.0003.
Values sent between devices are 32-bit elements; how exact they have to be, the bound alone decides.
A program may use at most 128 MiB of HBM per device.

v0:
```python
import functools

import jax
import jax.numpy as jnp
from jax import lax
from jax.experimental import pallas as pl
from jax.experimental.pallas import tpu as pltpu
from jax.sharding import PartitionSpec as P

F32, BF16 = jnp.float32, jnp.bfloat16
D, LAYERS, SLOTS, COLORS = 256, 4, 16, 3
GROUP = 128
NT = (((1,), (1,)), ((), ()))
NN = (((1,), (0,)), ((), ()))
TN = (((0,), (0,)), ((), ()))


def mm(a, b, dims):
    return lax.dot_general(a, b, dims, preferred_element_type=F32)


def split(v):
    hi = v.astype(BF16)
    return hi, (v - hi.astype(F32)).astype(BF16)


def left3(hi, lo, axis):
    return jnp.concatenate([hi, hi, lo], axis=axis)


def right3(hi, lo, axis):
    return jnp.concatenate([hi, lo, hi], axis=axis)


def silu_and_slope(pre):
    sig = jax.nn.sigmoid(pre)
    act = pre * sig
    return act, sig + act * (1.0 - sig)


def softplus(z):
    y = jnp.exp(-jnp.abs(z))
    s = y / (2.0 + y)
    q = s * s
    series = 1.0 / 17.0
    for odd in (15, 13, 11, 9, 7, 5, 3, 1):
        series = series * q + 1.0 / odd
    return jnp.maximum(z, 0.0) + 2.0 * s * series


def one_minus_exp(tau):
    series = 1.0
    for k in (7, 6, 5, 4, 3, 2):
        series = 1.0 - tau * series * (1.0 / k)
    return jnp.where(tau < 0.25, tau * series, 1.0 - jnp.exp(-tau))


def cumulative(v):
    rows = lax.broadcasted_iota(jnp.int32, v.shape, 0)
    for step in (1, 2, 4, 8):
        v = v + jnp.where(rows >= step, pltpu.roll(v, step, 0), 0.0)
    return v


def kernel(
    n_cell, x_hbm, sp_ref, cnt_ref, w_ref, head_ref, din_ref, dout_ref, cg_ref,
    lg_ref, hg_ref, ig_ref, og_ref, sg_hbm,
    x_ref, h_ref, s_ref, f_ref, dph_ref, dpl_ref,
    wt_ref, wb_ref, v_ref, dv_ref, dh_ref, headt_ref, dot_ref, pad_ref,
    z_ref, sm_ref, et_ref, hacc_ref,
    p_ref, pr_ref, t_ref, tr_ref, q_ref, qs_ref, px_ref, dpre_ref, ogs_ref,
    igs_ref, igr_ref, ex_ref, exc_ref, eb_ref, ef_ref, igf_ref,
    g_ref, cr_ref, half_ref, rr_ref, red_ref,
    x_sem, o_sem, e1_send, e1_recv, t_send, t_recv, e2_send, e2_recv,
    ig_send, ig_recv, ec_send, ec_recv, eb_send, eb_recv, ef_send, ef_recv, ia_send, ia_recv,
    c_send, c_recv, r_send, r_recv, a_send, a_recv, s_send, s_recv,
):
    me = lax.axis_index("cell")
    ray = lax.axis_index("rays")
    core = lax.rem(ray, 2)
    spot = ray // 2
    sibling = ray + 1 - 2 * core
    n_groups = sp_ref.shape[0] // GROUP
    n_spot = 8
    owned = GROUP // n_cell
    wide = 8 * GROUP
    my_rows = pl.ds(pl.multiple_of(me * owned, 8), owned)

    def take(g, side):
        part = pl.ds(g * GROUP * SLOTS, GROUP * SLOTS)
        lanes = pl.ds(side * 128, 128)
        return pltpu.make_async_copy(x_hbm.at[part, lanes], x_ref.at[side, part, :], x_sem.at[g, side])

    def give(g, side):
        part = pl.ds(g * GROUP * SLOTS, GROUP * SLOTS)
        lanes = pl.ds(side * 128, 128)
        return pltpu.make_async_copy(x_ref.at[side, part, :], sg_hbm.at[part, lanes], o_sem.at[g, side])

    for g in range(n_groups):
        for side in range(2):
            take(g, side).start()

    def cell_peer(d):
        return {"cell": lax.rem(me + d, n_cell)}

    def spot_peer(d):
        return {"rays": 2 * lax.rem(spot + d, n_spot) + core}

    barrier = pltpu.get_barrier_semaphore()

    def greet(d, _):
        pl.semaphore_signal(barrier, inc=1, device_id=cell_peer(d))
        pl.semaphore_signal(barrier, inc=1, device_id=spot_peer(d))
        return 0

    lax.fori_loop(1, n_cell, greet, 0)
    pl.semaphore_signal(barrier, inc=1, device_id={"rays": sibling})

    def remote(src, dst, send, recv, device):
        return pltpu.make_async_remote_copy(
            src_ref=src, dst_ref=dst, send_sem=send, recv_sem=recv, device_id=device
        )

    def each(count, make, act):
        def body(d, _):
            act(make(d))
            return 0

        lax.fori_loop(1, count, body, 0)

    def e1(g, d):
        to = lax.rem(me + d, n_cell)
        rows = pl.ds(pl.multiple_of(to * owned, 8), owned)
        return remote(p_ref.at[g, rows, :], pr_ref.at[g, me], e1_send.at[g, d], e1_recv.at[g, d], cell_peer(d))

    def t1(g, d):
        return remote(t_ref.at[g], tr_ref.at[g, me], t_send.at[g, d], t_recv.at[g, d], cell_peer(d))

    def e2(g, d):
        return remote(qs_ref.at[g], q_ref.at[g, my_rows, :], e2_send.at[g, d], e2_recv.at[g, d], cell_peer(d))

    def igc(d):
        to = lax.rem(me + d, n_cell)
        return remote(igs_ref.at[to], igr_ref.at[me], ig_send.at[d], ig_recv.at[d], cell_peer(d))

    ex_mine = pl.ds(pl.multiple_of(core * 24, 8), 24)
    ex_other = pl.ds(pl.multiple_of((1 - core) * 24, 8), 24)

    def ecc():
        return remote(ex_ref.at[ex_other, :], exc_ref, ec_send.at[0], ec_recv.at[0], {"rays": sibling})

    def ebc(d):
        return remote(eb_ref.at[spot], eb_ref.at[spot], eb_send.at[d], eb_recv.at[d], spot_peer(d))

    def efc():
        return remote(ef_ref.at[ex_mine, :], ef_ref.at[ex_mine, :], ef_send.at[0], ef_recv.at[0], {"rays": sibling})

    def iac(d):
        return remote(ef_ref.at[pl.ds(0, 32), :], igf_ref.at[me], ia_send.at[d], ia_recv.at[d], cell_peer(d))

    def cc(l):
        other = pl.ds(pl.multiple_of((1 - core) * 128, 128), 128)
        return remote(g_ref.at[l, other, :], cr_ref.at[l], c_send.at[l], c_recv.at[l], {"rays": sibling})

    def rc(l, d):
        to = lax.rem(spot + d, n_spot)
        rows = pl.ds(pl.multiple_of(to * 16, 16), 16)
        return remote(half_ref.at[l, rows, :], rr_ref.at[l, spot], r_send.at[l, d], r_recv.at[l, d], spot_peer(d))

    red_half = pl.ds(pl.multiple_of(core * 128, 128), 128)
    red_block = pl.ds(pl.multiple_of(core * 128 + spot * 16, 16), 16)

    def ac(l, d):
        return remote(red_ref.at[l, red_block, :], red_ref.at[l, red_block, :], a_send.at[l, d], a_recv.at[l, d], spot_peer(d))

    def sc(l):
        return remote(red_ref.at[l, red_half, :], red_ref.at[l, red_half, :], s_send.at[l], s_recv.at[l], {"rays": sibling})

    start = lambda c: c.start()
    arrived = lambda c: c.wait_recv()
    sent = lambda c: c.wait_send()

    for l in range(LAYERS):
        hi, lo = split(w_ref[l])
        wb_ref[l] = left3(hi, lo, 1)
        thi, tlo = split(w_ref[l].T)
        wt_ref[l] = left3(thi, tlo, 1)
        if l == 0:
            v_ref[...] = left3(thi, tlo, 0)
    headt_ref[...] = jnp.broadcast_to(head_ref[...], (GROUP, D)).T
    for g in range(n_groups):
        rays = pl.ds(g * GROUP, GROUP)
        pad_ref[...] = jnp.zeros_like(pad_ref)
        pad_ref[:, 0:SLOTS] = sp_ref[rays, :]
        spacing = pad_ref[...].T[0:SLOTS, :]
        count = jnp.broadcast_to(cnt_ref[rays, :].astype(F32), (GROUP, GROUP)).T[0:SLOTS, :]
        slot = lax.broadcasted_iota(jnp.int32, (SLOTS, GROUP), 0).astype(F32)
        sm_ref[g, 0] = jnp.where(slot < count, spacing, 0.0)

    def x_rows(g, s):
        return pl.ds(g * GROUP * SLOTS + s, GROUP, stride=SLOTS)

    def x_load(g, s):
        return jnp.concatenate([x_ref[side, x_rows(g, s), :] for side in range(2)], axis=1)

    def forward(g, half):
        chunk = 2 * g + half
        hidden = [None] * 4
        for q in range(4):
            slabs = [x_load(g, 8 * half + 2 * q + t) for t in range(2)]
            hidden[q] = right3(*split(jnp.concatenate(slabs, axis=0)), 1)
        for l in range(LAYERS):
            for q in range(4):
                columns = pl.ds(q * 2 * GROUP, 2 * GROUP)
                pre = mm(wt_ref[l], hidden[q], NT if l == 0 else NN)
                act, slope = silu_and_slope(pre)
                s_ref[l, chunk, :, columns] = slope
                if l < LAYERS - 1:
                    hi, lo = split(act)
                    h_ref[l, 0, chunk, :, columns] = hi
                    h_ref[l, 1, chunk, :, columns] = lo
                    hidden[q] = right3(hi, lo, 0)
                else:
                    f_ref[chunk, :, columns] = act
                    for t in range(2):
                        z = jnp.sum(act[:, t * GROUP:(t + 1) * GROUP] * headt_ref[...], axis=0, keepdims=True)
                        z_ref[g, pl.ds(8 * half + 2 * q + t, 1), :] = z

    def slot_of(ref, g, s):
        return ref[2 * g + s // 8, :, (s % 8) * GROUP:(s % 8 + 1) * GROUP]

    def rays_forward(g):
        z = z_ref[g]
        tau = softplus(z) * sm_ref[g, 0]
        incl = cumulative(tau)
        excl = incl - tau
        opaque = one_minus_exp(tau)
        sm_ref[g, 1] = tau
        sm_ref[g, 2] = excl
        sm_ref[g, 3] = opaque
        sm_ref[g, 4] = sm_ref[g, 0] * jax.nn.sigmoid(z)
        total = jnp.broadcast_to(incl[SLOTS - 1:SLOTS, :], (8, GROUP))
        t_ref[g] = total
        tr_ref[g, me] = total
        each(n_cell, functools.partial(t1, g), start)
        local = jnp.exp(-excl) * opaque
        acc = slot_of(f_ref, g, 0) * local[0:1, :]
        for s in range(1, SLOTS):
            acc = acc + slot_of(f_ref, g, s) * local[s:s + 1, :]
        p_ref[g] = acc.T
        each(n_cell, functools.partial(e1, g), start)
        pr_ref[g, me] = p_ref[g, my_rows, :]

    def decode(g):
        each(n_cell, functools.partial(t1, g), arrived)
        each(n_cell, functools.partial(e1, g), arrived)
        offset = jnp.zeros((1, GROUP), F32)
        own = jnp.zeros((1, GROUP), F32)
        rows = []
        for j in range(n_cell):
            rows.append(jnp.exp(-offset))
            own = jnp.where(me == j, offset, own)
            offset = offset + tr_ref[g, j][0:1, :]
        sm_ref[g, 5] = jnp.broadcast_to(own, (SLOTS, GROUP))
        et_ref[...] = jnp.concatenate(rows + [jnp.zeros((GROUP - n_cell, GROUP), F32)], axis=0).T
        et = et_ref[my_rows, :]
        parts = [pr_ref[g, j] * et[:, j:j + 1] for j in range(n_cell)]
        pixel = parts[0]
        for j in range(1, n_cell):
            pixel = pixel + parts[j]
        px_ref[g] = pixel
        pre = mm(right3(*split(pixel), 1), dv_ref[...], NN)
        colors = cg_ref[pl.ds(pl.multiple_of(g * GROUP + me * owned, 8), owned), :]
        act, slope = silu_and_slope(pre)
        reach = colors[:, 0:1] * dot_ref[0:1, :]
        for c in range(1, COLORS):
            reach = reach + colors[:, c:c + 1] * dot_ref[c:c + 1, :]
        dpre = reach * slope
        dpre_ref[g] = dpre
        for c in range(COLORS):
            ogs_ref[g, c:c + 1, :] = jnp.sum(act * colors[:, c:c + 1], axis=0, keepdims=True)
        grad = mm(right3(*split(dpre), 1), dh_ref[...], NT)
        lanes = lax.broadcasted_iota(jnp.int32, (owned, GROUP), 1)
        later = jnp.zeros((owned, GROUP), F32)
        for j in range(1, n_cell):
            value = jnp.sum(parts[j] * grad, axis=1, keepdims=True)
            later = later + jnp.where(lanes < j, value, 0.0)
        payload = jnp.concatenate([grad, later], axis=1)
        qs_ref[g] = payload
        each(n_cell, functools.partial(e2, g), start)
        q_ref[g, my_rows, :] = payload

    def decoder_grads():
        px = right3(*split(px_ref[...].reshape(n_groups * owned, D)), 0)
        dp = left3(*split(dpre_ref[...].reshape(n_groups * owned, D)), 0)
        grad = mm(px, dp, TN)
        colors = ogs_ref[0]
        for g in range(1, n_groups):
            colors = colors + ogs_ref[g]
        for j in range(n_cell):
            igs_ref[j, 0:32, :] = grad[32 * j:32 * j + 32, :]
            igs_ref[j, 32:40, :] = colors
        each(n_cell, igc, start)
        igr_ref[me] = igs_ref[me]

    def rays_backward(g):
        each(n_cell, functools.partial(e2, g), arrived)
        gradt = q_ref[g, :, 0:D].T
        latert = q_ref[g, :, D:D + GROUP].T[0:8, :]
        picked = lax.broadcasted_iota(jnp.int32, (8, GROUP), 0) == me
        later = jnp.sum(jnp.where(picked, latert, 0.0), axis=0, keepdims=True)
        et_ref[...] = jnp.zeros_like(et_ref)
        for s in range(SLOTS):
            et_ref[s:s + 1, :] = jnp.sum(slot_of(f_ref, g, s) * gradt, axis=0, keepdims=True)
        c = et_ref[0:SLOTS, :]
        tau = sm_ref[g, 1]
        trans = jnp.exp(-(sm_ref[g, 5] + sm_ref[g, 2]))
        weight = trans * sm_ref[g, 3]
        incl = cumulative(weight * c)
        after = later + incl[SLOTS - 1:SLOTS, :] - incl
        dz = sm_ref[g, 4] * (trans * jnp.exp(-tau) * c - after)
        sm_ref[g, 6] = weight
        sm_ref[g, 7] = dz
        q_ref[g, :, 0:GROUP] = gradt[0:GROUP, :]
        q_ref[g, :, GROUP:2 * GROUP] = gradt[GROUP:D, :]

    def head_step(chunk, l):
        g, half = chunk // 2, lax.rem(chunk, 2)
        for q in range(8):
            row = pl.ds(8 * half + q, 1)
            weight, dz = sm_ref[g, 6, row, :], sm_ref[g, 7, row, :]
            columns = pl.ds(q * GROUP, GROUP)
            for part in range(2):
                rows = pl.ds(part * 128, 128)
                back = q_ref[g, :, part * GROUP:(part + 1) * GROUP] * weight + headt_ref[rows, :] * dz
                hacc_ref[rows, :] += f_ref[chunk, rows, columns] * dz
                hi, lo = split(back * s_ref[LAYERS - 1, chunk, rows, columns])
                dph_ref[chunk, rows, columns] = hi
                dpl_ref[chunk, rows, columns] = lo

    def layer_step(chunk, l):
        hi, lo = dph_ref[chunk], dpl_ref[chunk]
        source = right3(h_ref[l - 1, 0, chunk], h_ref[l - 1, 1, chunk], 1)
        g_ref[l] += mm(source, left3(hi, lo, 1), NT)
        for q in range(4):
            columns = slice(q * 2 * GROUP, (q + 1) * 2 * GROUP)
            back = mm(wb_ref[l], right3(hi[:, columns], lo[:, columns], 0), NN)
            nhi, nlo = split(back * s_ref[l - 1, chunk, :, columns])
            dph_ref[chunk, :, columns] = nhi
            dpl_ref[chunk, :, columns] = nlo

    def first_grad(chunk):
        g, half = chunk // 2, lax.rem(chunk, 2)
        rows = jnp.concatenate([x_load(g, 8 * half + q) for q in range(8)], axis=0)
        g_ref[0] += mm(left3(dph_ref[chunk], dpl_ref[chunk], 1), right3(*split(rows), 0), NN)

    def first_back(chunk):
        g, half = chunk // 2, lax.rem(chunk, 2)
        for q in range(4):
            columns = slice(q * 2 * GROUP, (q + 1) * 2 * GROUP)
            back = mm(right3(dph_ref[chunk, :, columns], dpl_ref[chunk, :, columns], 0), v_ref[...], TN)
            for t in range(2):
                for side in range(2):
                    x_ref[side, x_rows(g, 8 * half + 2 * q + t), :] = back[
                        t * GROUP:(t + 1) * GROUP, side * 128:(side + 1) * 128
                    ]

    def sum_a(l):
        cc(l).start()

    def sum_b(l):
        cc(l).wait_recv()
        half_ref[l] = g_ref[l, red_half, :] + cr_ref[l]
        each(n_spot, functools.partial(rc, l), start)
        rr_ref[l, spot] = half_ref[l, pl.ds(pl.multiple_of(spot * 16, 16), 16), :]

    def sum_c(l):
        each(n_spot, functools.partial(rc, l), arrived)
        total = rr_ref[l, 0]
        for j in range(1, n_spot):
            total = total + rr_ref[l, j]
        red_ref[l, red_block, :] = total
        each(n_spot, functools.partial(ac, l), start)

    def sum_d(l):
        each(n_spot, functools.partial(ac, l), arrived)
        sc(l).start()

    def sum_e(l):
        sc(l).wait_recv()
        lg_ref[l] = red_ref[l]

    def extra_a():
        each(n_cell, igc, arrived)
        total = igr_ref[0]
        for j in range(1, n_cell):
            total = total + igr_ref[j]
        ex_ref[0:40, :] = total
        ex_ref[40:48, :] = jnp.broadcast_to(jnp.sum(hacc_ref[...].T, axis=0, keepdims=True), (8, D))
        ecc().start()

    def extra_b():
        ecc().wait_recv()
        eb_ref[spot] = ex_ref[ex_mine, :] + exc_ref[...]
        each(n_spot, ebc, start)

    def extra_c():
        each(n_spot, ebc, arrived)
        total = eb_ref[0]
        for j in range(1, n_spot):
            total = total + eb_ref[j]
        ef_ref[ex_mine, :] = total
        efc().start()

    def extra_d():
        efc().wait_recv()
        each(n_cell, iac, start)
        igf_ref[me] = ef_ref[0:32, :]

    def extra_e():
        each(n_cell, iac, arrived)
        ig_ref[...] = igf_ref[...].reshape(D, D)
        pad_ref[...] = jnp.zeros_like(pad_ref)
        for part in range(2):
            pad_ref[0:8, :] = ef_ref[32:40, part * 128:(part + 1) * 128]
            og_ref[part * 128:(part + 1) * 128, :] = pad_ref[...].T[:, 0:COLORS]
        hg_ref[...] = ef_ref[40:41, :]

    def wait_x(g):
        for side in range(2):
            take(g, side).wait()

    def forward_loop(g):
        def body(half, _):
            forward(g, half)
            return 0

        lax.fori_loop(0, 2, body, 0)

    wait_x(0)
    forward_loop(0)
    pl.semaphore_wait(barrier, 2 * (n_cell - 1) + 1)
    rays_forward(0)
    hi, lo = split(din_ref[...])
    dv_ref[...] = left3(hi, lo, 0)
    dh_ref[...] = left3(hi, lo, 1)
    for part in range(2):
        pad_ref[...] = jnp.zeros_like(pad_ref)
        pad_ref[:, 0:COLORS] = dout_ref[part * 128:(part + 1) * 128, :]
        dot_ref[:, part * 128:(part + 1) * 128] = pad_ref[...].T[0:8, :]
    ogs_ref[...] = jnp.zeros_like(ogs_ref)
    g_ref[...] = jnp.zeros_like(g_ref)
    hacc_ref[...] = jnp.zeros_like(hacc_ref)
    wait_x(1)
    forward_loop(1)
    decode(0)
    rays_forward(1)
    rays_backward(0)

    def top(chunk, _):
        head_step(chunk, LAYERS - 1)
        layer_step(chunk, LAYERS - 1)
        return 0

    lax.fori_loop(0, 2, top, 0)
    decode(1)
    decoder_grads()
    rays_backward(1)
    lax.fori_loop(2, 4, top, 0)
    sum_a(3)
    extra_a()

    def middle(l):
        def body(chunk, _):
            layer_step(chunk, l)
            return 0

        return body

    lax.fori_loop(0, 2, middle(2), 0)
    sum_b(3)
    extra_b()
    lax.fori_loop(2, 4, middle(2), 0)
    sum_a(2)
    sum_c(3)
    extra_c()
    lax.fori_loop(0, 2, middle(1), 0)
    sum_b(2)
    sum_d(3)
    extra_d()
    lax.fori_loop(2, 4, middle(1), 0)
    sum_a(1)
    sum_c(2)
    sum_e(3)

    def first(chunk, _):
        first_grad(chunk)
        return 0

    lax.fori_loop(0, 2, first, 0)
    sum_b(1)
    sum_d(2)
    lax.fori_loop(2, 4, first, 0)
    g_ref[0] = g_ref[0].T
    sum_a(0)
    sum_c(1)
    sum_e(2)

    def last(chunk, _):
        first_back(chunk)
        return 0

    lax.fori_loop(0, 2, last, 0)
    for side in range(2):
        give(0, side).start()
    sum_b(0)
    sum_d(1)
    lax.fori_loop(2, 4, last, 0)
    for side in range(2):
        give(1, side).start()
    sum_c(0)
    sum_e(1)
    extra_e()
    sum_d(0)
    sum_e(0)
    for g in range(n_groups):
        for side in range(2):
            give(g, side).wait()
    for g in range(n_groups):
        each(n_cell, functools.partial(t1, g), sent)
        each(n_cell, functools.partial(e1, g), sent)
        each(n_cell, functools.partial(e2, g), sent)
    each(n_cell, igc, sent)
    ecc().wait_send()
    each(n_spot, ebc, sent)
    efc().wait_send()
    each(n_cell, iac, sent)
    for l in range(LAYERS):
        cc(l).wait_send()
        each(n_spot, functools.partial(rc, l), sent)
        each(n_spot, functools.partial(ac, l), sent)
        sc(l).wait_send()


def local(n_cell, encodings, spacing, counts, cell_weights, density_head, decoder_in, decoder_out, color_grad):
    rays, slots, width = encodings.shape
    rows = rays * slots
    groups, chunks, wide = rays // GROUP, rows // (8 * GROUP), 8 * GROUP
    owned = GROUP // n_cell
    vmem = pl.BlockSpec(memory_space=pltpu.VMEM)
    anywhere = pl.BlockSpec(memory_space=pl.ANY)
    dma = pltpu.SemaphoreType.DMA
    V = pltpu.VMEM
    scratch = [
        V((2, rows, 128), F32),
        V((LAYERS - 1, 2, chunks, D, wide), BF16),
        V((LAYERS, chunks, D, wide), F32),
        V((chunks, D, wide), F32),
        V((chunks, D, wide), BF16),
        V((chunks, D, wide), BF16),
        V((LAYERS, D, 3 * D), BF16),
        V((LAYERS, D, 3 * D), BF16),
        V((3 * D, D), BF16),
        V((3 * D, D), BF16),
        V((D, 3 * D), BF16),
        V((D, GROUP), F32),
        V((8, D), F32),
        V((GROUP, GROUP), F32),
        V((groups, SLOTS, GROUP), F32),
        V((groups, 8, SLOTS, GROUP), F32),
        V((GROUP, GROUP), F32),
        V((D, GROUP), F32),
        V((groups, GROUP, D), F32),
        V((groups, n_cell, owned, D), F32),
        V((groups, 8, GROUP), F32),
        V((groups, n_cell, 8, GROUP), F32),
        V((groups, GROUP, D + GROUP), F32),
        V((groups, owned, D + GROUP), F32),
        V((groups, owned, D), F32),
        V((groups, owned, D), F32),
        V((groups, 8, D), F32),
        V((n_cell, 40, D), F32),
        V((n_cell, 40, D), F32),
        V((48, D), F32),
        V((24, D), F32),
        V((8, 24, D), F32),
        V((48, D), F32),
        V((n_cell, 32, D), F32),
        V((LAYERS, D, D), F32),
        V((LAYERS, 128, D), F32),
        V((LAYERS, 128, D), F32),
        V((LAYERS, 8, 16, D), F32),
        V((LAYERS, D, D), F32),
        dma((groups, 2)), dma((groups, 2)),
        dma((groups, n_cell)), dma((groups, n_cell)),
        dma((groups, n_cell)), dma((groups, n_cell)),
        dma((groups, n_cell)), dma((groups, n_cell)),
        dma((n_cell,)), dma((n_cell,)),
        dma((1,)), dma((1,)),
        dma((8,)), dma((8,)),
        dma((1,)), dma((1,)),
        dma((n_cell,)), dma((n_cell,)),
        dma((LAYERS,)), dma((LAYERS,)),
        dma((LAYERS, 8)), dma((LAYERS, 8)),
        dma((LAYERS, 8)), dma((LAYERS, 8)),
        dma((LAYERS,)), dma((LAYERS,)),
    ]
    layer, head, din, dout, sample = pl.pallas_call(
        functools.partial(kernel, n_cell),
        out_shape=[
            jax.ShapeDtypeStruct((LAYERS, D, D), F32),
            jax.ShapeDtypeStruct((1, D), F32),
            jax.ShapeDtypeStruct((D, D), F32),
            jax.ShapeDtypeStruct((D, COLORS), F32),
            jax.ShapeDtypeStruct((rows, D), F32),
        ],
        in_specs=[anywhere] + [vmem] * 7,
        out_specs=[vmem] * 4 + [anywhere],
        scratch_shapes=scratch,
        compiler_params=pltpu.CompilerParams(
            collective_id=0, has_side_effects=True, vmem_limit_bytes=62 << 20
        ),
    )(
        encodings.reshape(rows, width), spacing, counts, cell_weights[0], density_head,
        decoder_in, decoder_out, color_grad,
    )
    return layer[None], head, din, dout, sample.reshape(rays, slots, width)


def solution(mesh):
    return jax.shard_map(
        functools.partial(local, mesh.shape["cell"]),
        mesh=mesh,
        in_specs=(
            P("rays", "cell", None), P("rays", "cell"), P("rays", "cell"), P("cell", None, None, None),
            P("cell", None), P(None, None), P(None, None), P("rays", None),
        ),
        out_specs=(
            P("cell", None, None, None), P("cell", None), P(None, None), P(None, None), P("rays", "cell", None),
        ),
        check_vma=False,
    )
```

profile of v0, /device:TPU:1, one launch (start us, length us, event | category | flops | bytes accessed | tf_op | source)
XLA Modules:
  0.0 96.9 jit_solution(8697065782695820724)
XLA Ops:
  0.6 1.5 %copy.13.sp_ref = f32[256,16]{1,0:T(8,128)} copy(f32[256,16]{0,1:T(8,128)} %param.9) | data formatting | bytes 32768 | tf_op args[1]
  2.1 1.5 %copy.14.cnt_ref = s32[256,1]{1,0:T(8,128)} copy(s32[256,1]{0,1:T(1,128)} %param.10) | data formatting | bytes 2048 | tf_op args[2]
  3.6 1.5 %copy.15.dout_ref = f32[256,3]{1,0:T(8,128)} copy(f32[256,3]{0,1:T(4,128)} %param.14) | data formatting | bytes 6144 | tf_op args[6]
  5.1 1.5 %copy.16.cg_ref = f32[256,3]{1,0:T(8,128)} copy(f32[256,3]{0,1:T(4,128)} %param.15) | data formatting | bytes 6144 | tf_op args[7]
  6.6 79.0 %shard_map.119 = (f32[4,256,256]{2,1,0:T(8,128)}, f32[1,256]{1,0:T(1,128)}, f32[256,256]{1,0:T(8,128)}, f32[256,3]{1,0:T(8,128)}, f32[4096,256]{1,0:T(8,128)}) custom-call(f32[4096,256]{1,0:T(8,128)} %bitcast.4, f32[256,16]{1,0:T(8,128)} %copy.13.sp_ref, s32[256,1]{1,0:T(8,128)} %copy.14.cnt_ref, f32[4,256,256]{2,1,0:T(8,128)} %bitcast.6, ...), custom_call_target="tpu_custom_call" | custom-call | tf_op jit(solution)/shard_map/pallas_call | solution.py:608
  85.6 1.6 %copy.17 = f32[256,3]{0,1:T(4,128)} copy(f32[256,3]{1,0:T(8,128)} %get-tuple-element.18) | data formatting | bytes 6144
  87.1 2.3 %copy.22 = f32[1,4,256,256]{3,2,1,0:T(8,128)} copy(f32[1,4,256,256]{3,2,1,0:T(8,128)} %bitcast.7) | data formatting | bytes 2097152
  89.4 1.2 %copy.23 = f32[1,256]{1,0:T(1,128)} copy(f32[1,256]{1,0:T(1,128)} %get-tuple-element.26) | data formatting | bytes 2048
  90.6 1.7 %copy.24 = f32[256,256]{1,0:T(8,128)} copy(f32[256,256]{1,0:T(8,128)} %get-tuple-element.27) | data formatting | bytes 524288
  92.3 4.6 %copy.25 = f32[256,16,256]{2,1,0:T(8,128)} copy(f32[256,16,256]{2,1,0:T(8,128)} %bitcast.5) | data formatting | bytes 8388608
where the time goes:
time: 97.3 us; the launch traced here: 96.9 us
  Pallas kernels  79 us (81%)
  local copies, waits for them, and re-layouts  17.3 us (18%)
    pallas_call x1, Pallas kernels, local(): pl.pallas_call(functools.partial(kernel, n_cell), out_shape=[jax.ShapeDty...  79 us
    unnamed x9, local copies, waits for them, and re-layouts  17.3 us

commit v1 on v0

--- a/solution.py
+++ b/solution.py
@@ -63,15 +63,16 @@
 
 
 def kernel(
-    n_cell, x_hbm, sp_ref, cnt_ref, w_ref, head_ref, din_ref, dout_ref, cg_ref,
-    lg_ref, hg_ref, ig_ref, og_ref, sg_hbm,
-    x_ref, h_ref, s_ref, f_ref, dph_ref, dpl_ref,
-    wt_ref, wb_ref, v_ref, dv_ref, dh_ref, headt_ref, dot_ref, pad_ref,
+    n_cell, x_hbm, sp_hbm, cnt_hbm, w_hbm, head_hbm, din_hbm, dout_hbm, cg_hbm,
+    red_ref, hg_ref, igf_ref, og_ref, x_ref,
+    sp_ref, cnt_ref, w_ref, head_ref, din_ref, dout_ref, cg_ref, cgt_ref,
+    h_ref, s_ref, f_ref, dph_ref, dpl_ref,
+    wt_ref, wb_ref, v_ref, dv_ref, dh_ref, headt_ref,
     z_ref, sm_ref, et_ref, hacc_ref,
     p_ref, pr_ref, t_ref, tr_ref, q_ref, qs_ref, px_ref, dpre_ref, ogs_ref,
-    igs_ref, igr_ref, ex_ref, exc_ref, eb_ref, ef_ref, igf_ref,
-    g_ref, cr_ref, half_ref, rr_ref, red_ref,
-    x_sem, o_sem, e1_send, e1_recv, t_send, t_recv, e2_send, e2_recv,
+    igs_ref, igr_ref, ex_ref, exc_ref, eb_ref, ef_ref,
+    g_ref, cr_ref, half_ref, rr_ref,
+    x_sem, in_sem, e1_send, e1_recv, t_send, t_recv, e2_send, e2_recv,
     ig_send, ig_recv, ec_send, ec_recv, eb_send, eb_recv, ef_send, ef_recv, ia_send, ia_recv,
     c_send, c_recv, r_send, r_recv, a_send, a_recv, s_send, s_recv,
 ):
@@ -80,7 +81,7 @@
     core = lax.rem(ray, 2)
     spot = ray // 2
     sibling = ray + 1 - 2 * core
-    n_groups = sp_ref.shape[0] // GROUP
+    n_groups = sp_ref.shape[1] // GROUP
     n_spot = 8
     owned = GROUP // n_cell
     wide = 8 * GROUP
@@ -91,14 +92,21 @@
         lanes = pl.ds(side * 128, 128)
         return pltpu.make_async_copy(x_hbm.at[part, lanes], x_ref.at[side, part, :], x_sem.at[g, side])
 
-    def give(g, side):
-        part = pl.ds(g * GROUP * SLOTS, GROUP * SLOTS)
-        lanes = pl.ds(side * 128, 128)
-        return pltpu.make_async_copy(x_ref.at[side, part, :], sg_hbm.at[part, lanes], o_sem.at[g, side])
-
+    pairs = (
+        (head_hbm, head_ref), (sp_hbm, sp_ref), (cnt_hbm, cnt_ref), (cg_hbm, cg_ref), (dout_hbm, dout_ref),
+        (din_hbm, din_ref),
+    )
+    small = [pltpu.make_async_copy(src, dst, in_sem.at[n]) for n, (src, dst) in enumerate(pairs)]
+    weights = [
+        pltpu.make_async_copy(w_hbm.at[l], w_ref.at[l], in_sem.at[len(pairs) + l]) for l in range(LAYERS)
+    ]
+    weights[0].start()
     for g in range(n_groups):
         for side in range(2):
             take(g, side).start()
+        if g == 0:
+            for c in weights[1:] + small:
+                c.start()
 
     def cell_peer(d):
         return {"cell": lax.rem(me + d, n_cell)}
@@ -121,9 +129,9 @@
             src_ref=src, dst_ref=dst, send_sem=send, recv_sem=recv, device_id=device
         )
 
-    def each(count, make, act):
+    def each(count, make):
         def body(d, _):
-            act(make(d))
+            make(d).start()
             return 0
 
         lax.fori_loop(1, count, body, 0)
@@ -131,17 +139,33 @@
     def e1(g, d):
         to = lax.rem(me + d, n_cell)
         rows = pl.ds(pl.multiple_of(to * owned, 8), owned)
-        return remote(p_ref.at[g, rows, :], pr_ref.at[g, me], e1_send.at[g, d], e1_recv.at[g, d], cell_peer(d))
+        return remote(p_ref.at[g, rows, :], pr_ref.at[g, me], e1_send.at[g], e1_recv.at[g], cell_peer(d))
+
+    def e1_all(g):
+        blocks = pr_ref.at[g, pl.ds(0, n_cell - 1)]
+        return remote(blocks, blocks, e1_send.at[g], e1_recv.at[g], cell_peer(1))
 
     def t1(g, d):
-        return remote(t_ref.at[g], tr_ref.at[g, me], t_send.at[g, d], t_recv.at[g, d], cell_peer(d))
+        return remote(t_ref.at[g], tr_ref.at[g, me], t_send.at[g], t_recv.at[g], cell_peer(d))
+
+    def t1_all(g):
+        blocks = tr_ref.at[g, pl.ds(0, n_cell - 1)]
+        return remote(blocks, blocks, t_send.at[g], t_recv.at[g], cell_peer(1))
 
     def e2(g, d):
-        return remote(qs_ref.at[g], q_ref.at[g, my_rows, :], e2_send.at[g, d], e2_recv.at[g, d], cell_peer(d))
+        return remote(qs_ref.at[g], q_ref.at[g, my_rows, :], e2_send.at[g], e2_recv.at[g], cell_peer(d))
+
+    def e2_all(g):
+        blocks = q_ref.at[g, pl.ds(0, GROUP - owned), :]
+        return remote(blocks, blocks, e2_send.at[g], e2_recv.at[g], cell_peer(1))
 
     def igc(d):
         to = lax.rem(me + d, n_cell)
-        return remote(igs_ref.at[to], igr_ref.at[me], ig_send.at[d], ig_recv.at[d], cell_peer(d))
+        return remote(igs_ref.at[to], igr_ref.at[me], ig_send.at[0], ig_recv.at[0], cell_peer(d))
+
+    def igc_all():
+        blocks = igr_ref.at[pl.ds(0, n_cell - 1)]
+        return remote(blocks, blocks, ig_send.at[0], ig_recv.at[0], cell_peer(1))
 
     ex_mine = pl.ds(pl.multiple_of(core * 24, 8), 24)
     ex_other = pl.ds(pl.multiple_of((1 - core) * 24, 8), 24)
@@ -150,13 +174,21 @@
         return remote(ex_ref.at[ex_other, :], exc_ref, ec_send.at[0], ec_recv.at[0], {"rays": sibling})
 
     def ebc(d):
-        return remote(eb_ref.at[spot], eb_ref.at[spot], eb_send.at[d], eb_recv.at[d], spot_peer(d))
+        return remote(eb_ref.at[spot], eb_ref.at[spot], eb_send.at[0], eb_recv.at[0], spot_peer(d))
+
+    def ebc_all():
+        blocks = eb_ref.at[pl.ds(0, n_spot - 1)]
+        return remote(blocks, blocks, eb_send.at[0], eb_recv.at[0], spot_peer(1))
 
     def efc():
         return remote(ef_ref.at[ex_mine, :], ef_ref.at[ex_mine, :], ef_send.at[0], ef_recv.at[0], {"rays": sibling})
 
     def iac(d):
-        return remote(ef_ref.at[pl.ds(0, 32), :], igf_ref.at[me], ia_send.at[d], ia_recv.at[d], cell_peer(d))
+        return remote(ef_ref.at[pl.ds(0, 32), :], igf_ref.at[me], ia_send.at[0], ia_recv.at[0], cell_peer(d))
+
+    def iac_all():
+        blocks = igf_ref.at[pl.ds(0, n_cell - 1)]
+        return remote(blocks, blocks, ia_send.at[0], ia_recv.at[0], cell_peer(1))
 
     def cc(l):
         other = pl.ds(pl.multiple_of((1 - core) * 128, 128), 128)
@@ -165,37 +197,54 @@
     def rc(l, d):
         to = lax.rem(spot + d, n_spot)
         rows = pl.ds(pl.multiple_of(to * 16, 16), 16)
-        return remote(half_ref.at[l, rows, :], rr_ref.at[l, spot], r_send.at[l, d], r_recv.at[l, d], spot_peer(d))
+        return remote(half_ref.at[l, rows, :], rr_ref.at[l, spot], r_send.at[l], r_recv.at[l], spot_peer(d))
+
+    def rc_all(l):
+        blocks = rr_ref.at[l, pl.ds(0, n_spot - 1)]
+        return remote(blocks, blocks, r_send.at[l], r_recv.at[l], spot_peer(1))
 
     red_half = pl.ds(pl.multiple_of(core * 128, 128), 128)
     red_block = pl.ds(pl.multiple_of(core * 128 + spot * 16, 16), 16)
 
     def ac(l, d):
-        return remote(red_ref.at[l, red_block, :], red_ref.at[l, red_block, :], a_send.at[l, d], a_recv.at[l, d], spot_peer(d))
+        return remote(red_ref.at[l, red_block, :], red_ref.at[l, red_block, :], a_send.at[l], a_recv.at[l], spot_peer(d))
+
+    def ac_all(l):
+        blocks = red_ref.at[l, pl.ds(0, 112), :]
+        return remote(blocks, blocks, a_send.at[l], a_recv.at[l], spot_peer(1))
 
     def sc(l):
         return remote(red_ref.at[l, red_half, :], red_ref.at[l, red_half, :], s_send.at[l], s_recv.at[l], {"rays": sibling})
 
-    start = lambda c: c.start()
-    arrived = lambda c: c.wait_recv()
-    sent = lambda c: c.wait_send()
-
-    for l in range(LAYERS):
-        hi, lo = split(w_ref[l])
-        wb_ref[l] = left3(hi, lo, 1)
+    def forward_weights(l):
+        weights[l].wait()
         thi, tlo = split(w_ref[l].T)
         wt_ref[l] = left3(thi, tlo, 1)
         if l == 0:
             v_ref[...] = left3(thi, tlo, 0)
-    headt_ref[...] = jnp.broadcast_to(head_ref[...], (GROUP, D)).T
-    for g in range(n_groups):
-        rays = pl.ds(g * GROUP, GROUP)
-        pad_ref[...] = jnp.zeros_like(pad_ref)
-        pad_ref[:, 0:SLOTS] = sp_ref[rays, :]
-        spacing = pad_ref[...].T[0:SLOTS, :]
-        count = jnp.broadcast_to(cnt_ref[rays, :].astype(F32), (GROUP, GROUP)).T[0:SLOTS, :]
-        slot = lax.broadcasted_iota(jnp.int32, (SLOTS, GROUP), 0).astype(F32)
-        sm_ref[g, 0] = jnp.where(slot < count, spacing, 0.0)
+
+    def backward_weights():
+        for l in range(1, LAYERS):
+            wb_ref[l] = left3(*split(w_ref[l]), 1)
+
+    def ray_inputs():
+        for c in small:
+            c.wait()
+        headt_ref[...] = jnp.broadcast_to(head_ref[...], (GROUP, D)).T
+        slot = lax.broadcasted_iota(jnp.int32, (SLOTS, GROUP), 0)
+        for g in range(n_groups):
+            rays = slice(g * GROUP, (g + 1) * GROUP)
+            sm_ref[g, 0] = jnp.where(slot < cnt_ref[:, rays], sp_ref[:, rays], 0.0)
+
+    def decoder_inputs():
+        hi, lo = split(din_ref[...])
+        dv_ref[...] = left3(hi, lo, 0)
+        dh_ref[...] = left3(hi, lo, 1)
+        ogs_ref[...] = jnp.zeros_like(ogs_ref)
+        for g in range(n_groups):
+            et_ref[...] = jnp.zeros_like(et_ref)
+            et_ref[0:COLORS, :] = cg_ref[:, g * GROUP:(g + 1) * GROUP]
+            cgt_ref[g] = et_ref[...].T
 
     def x_rows(g, s):
         return pl.ds(g * GROUP * SLOTS + s, GROUP, stride=SLOTS)
@@ -242,18 +291,18 @@
         total = jnp.broadcast_to(incl[SLOTS - 1:SLOTS, :], (8, GROUP))
         t_ref[g] = total
         tr_ref[g, me] = total
-        each(n_cell, functools.partial(t1, g), start)
+        each(n_cell, functools.partial(t1, g))
         local = jnp.exp(-excl) * opaque
         acc = slot_of(f_ref, g, 0) * local[0:1, :]
         for s in range(1, SLOTS):
             acc = acc + slot_of(f_ref, g, s) * local[s:s + 1, :]
         p_ref[g] = acc.T
-        each(n_cell, functools.partial(e1, g), start)
+        each(n_cell, functools.partial(e1, g))
         pr_ref[g, me] = p_ref[g, my_rows, :]
 
     def decode(g):
-        each(n_cell, functools.partial(t1, g), arrived)
-        each(n_cell, functools.partial(e1, g), arrived)
+        t1_all(g).wait_recv()
+        e1_all(g).wait_recv()
         offset = jnp.zeros((1, GROUP), F32)
         own = jnp.zeros((1, GROUP), F32)
         rows = []
@@ -270,11 +319,11 @@
             pixel = pixel + parts[j]
         px_ref[g] = pixel
         pre = mm(right3(*split(pixel), 1), dv_ref[...], NN)
-        colors = cg_ref[pl.ds(pl.multiple_of(g * GROUP + me * owned, 8), owned), :]
+        colors = cgt_ref[g, my_rows, :]
         act, slope = silu_and_slope(pre)
-        reach = colors[:, 0:1] * dot_ref[0:1, :]
+        reach = colors[:, 0:1] * dout_ref[0:1, :]
         for c in range(1, COLORS):
-            reach = reach + colors[:, c:c + 1] * dot_ref[c:c + 1, :]
+            reach = reach + colors[:, c:c + 1] * dout_ref[c:c + 1, :]
         dpre = reach * slope
         dpre_ref[g] = dpre
         for c in range(COLORS):
@@ -287,7 +336,7 @@
             later = later + jnp.where(lanes < j, value, 0.0)
         payload = jnp.concatenate([grad, later], axis=1)
         qs_ref[g] = payload
-        each(n_cell, functools.partial(e2, g), start)
+        each(n_cell, functools.partial(e2, g))
         q_ref[g, my_rows, :] = payload
 
     def decoder_grads():
@@ -300,11 +349,11 @@
         for j in range(n_cell):
             igs_ref[j, 0:32, :] = grad[32 * j:32 * j + 32, :]
             igs_ref[j, 32:40, :] = colors
-        each(n_cell, igc, start)
+        each(n_cell, igc)
         igr_ref[me] = igs_ref[me]
 
     def rays_backward(g):
-        each(n_cell, functools.partial(e2, g), arrived)
+        e2_all(g).wait_recv()
         gradt = q_ref[g, :, 0:D].T
         latert = q_ref[g, :, D:D + GROUP].T[0:8, :]
         picked = lax.broadcasted_iota(jnp.int32, (8, GROUP), 0) == me
@@ -371,27 +420,26 @@
     def sum_b(l):
         cc(l).wait_recv()
         half_ref[l] = g_ref[l, red_half, :] + cr_ref[l]
-        each(n_spot, functools.partial(rc, l), start)
+        each(n_spot, functools.partial(rc, l))
         rr_ref[l, spot] = half_ref[l, pl.ds(pl.multiple_of(spot * 16, 16), 16), :]
 
     def sum_c(l):
-        each(n_spot, functools.partial(rc, l), arrived)
+        rc_all(l).wait_recv()
         total = rr_ref[l, 0]
         for j in range(1, n_spot):
             total = total + rr_ref[l, j]
         red_ref[l, red_block, :] = total
-        each(n_spot, functools.partial(ac, l), start)
+        each(n_spot, functools.partial(ac, l))
 
     def sum_d(l):
-        each(n_spot, functools.partial(ac, l), arrived)
+        ac_all(l).wait_recv()
         sc(l).start()
 
     def sum_e(l):
         sc(l).wait_recv()
-        lg_ref[l] = red_ref[l]
 
     def extra_a():
-        each(n_cell, igc, arrived)
+        igc_all().wait_recv()
         total = igr_ref[0]
         for j in range(1, n_cell):
             total = total + igr_ref[j]
@@ -402,10 +450,10 @@
     def extra_b():
         ecc().wait_recv()
         eb_ref[spot] = ex_ref[ex_mine, :] + exc_ref[...]
-        each(n_spot, ebc, start)
+        each(n_spot, ebc)
 
     def extra_c():
-        each(n_spot, ebc, arrived)
+        ebc_all().wait_recv()
         total = eb_ref[0]
         for j in range(1, n_spot):
             total = total + eb_ref[j]
@@ -414,16 +462,12 @@
 
     def extra_d():
         efc().wait_recv()
-        each(n_cell, iac, start)
+        each(n_cell, iac)
         igf_ref[me] = ef_ref[0:32, :]
 
     def extra_e():
-        each(n_cell, iac, arrived)
-        ig_ref[...] = igf_ref[...].reshape(D, D)
-        pad_ref[...] = jnp.zeros_like(pad_ref)
-        for part in range(2):
-            pad_ref[0:8, :] = ef_ref[32:40, part * 128:(part + 1) * 128]
-            og_ref[part * 128:(part + 1) * 128, :] = pad_ref[...].T[:, 0:COLORS]
+        iac_all().wait_recv()
+        og_ref[...] = ef_ref[32:32 + COLORS, :]
         hg_ref[...] = ef_ref[40:41, :]
 
     def wait_x(g):
@@ -437,109 +481,104 @@
 
         lax.fori_loop(0, 2, body, 0)
 
+    def rest(first_chunk, step):
+        def body(chunk, _):
+            step(chunk)
+            return 0
+
+        lax.fori_loop(first_chunk, first_chunk + 2, body, 0)
+
+    def top(chunk):
+        head_step(chunk, LAYERS - 1)
+        layer_step(chunk, LAYERS - 1)
+
+    middle = [functools.partial(layer_step, l=l) for l in range(LAYERS)]
+    forward_weights(0)
+    ray_inputs()
+    for l in range(1, LAYERS):
+        forward_weights(l)
     wait_x(0)
     forward_loop(0)
     pl.semaphore_wait(barrier, 2 * (n_cell - 1) + 1)
     rays_forward(0)
-    hi, lo = split(din_ref[...])
-    dv_ref[...] = left3(hi, lo, 0)
-    dh_ref[...] = left3(hi, lo, 1)
-    for part in range(2):
-        pad_ref[...] = jnp.zeros_like(pad_ref)
-        pad_ref[:, 0:COLORS] = dout_ref[part * 128:(part + 1) * 128, :]
-        dot_ref[:, part * 128:(part + 1) * 128] = pad_ref[...].T[0:8, :]
-    ogs_ref[...] = jnp.zeros_like(ogs_ref)
+    wait_x(1)
+    forward_loop(1)
+    rays_forward(1)
+    decoder_inputs()
+    decode(0)
+    backward_weights()
     g_ref[...] = jnp.zeros_like(g_ref)
     hacc_ref[...] = jnp.zeros_like(hacc_ref)
-    wait_x(1)
-    forward_loop(1)
-    decode(0)
-    rays_forward(1)
     rays_backward(0)
-
-    def top(chunk, _):
-        head_step(chunk, LAYERS - 1)
-        layer_step(chunk, LAYERS - 1)
-        return 0
-
-    lax.fori_loop(0, 2, top, 0)
+    rest(0, top)
     decode(1)
+    rest(0, middle[2])
     decoder_grads()
+    rest(0, middle[1])
     rays_backward(1)
-    lax.fori_loop(2, 4, top, 0)
+    rest(2, top)
     sum_a(3)
     extra_a()
-
-    def middle(l):
-        def body(chunk, _):
-            layer_step(chunk, l)
-            return 0
-
-        return body
-
-    lax.fori_loop(0, 2, middle(2), 0)
+    rest(2, middle[2])
     sum_b(3)
     extra_b()
-    lax.fori_loop(2, 4, middle(2), 0)
     sum_a(2)
+    rest(2, middle[1])
+    sum_b(2)
+    sum_a(1)
+    rest(0, first_grad)
+    sum_b(1)
+    rest(2, first_grad)
+    g_ref[0] = g_ref[0].T
+    sum_a(0)
     sum_c(3)
     extra_c()
-    lax.fori_loop(0, 2, middle(1), 0)
-    sum_b(2)
+    rest(0, first_back)
+    sum_b(0)
+    sum_c(2)
+    extra_d()
+    rest(2, first_back)
+    sum_c(1)
     sum_d(3)
-    extra_d()
-    lax.fori_loop(2, 4, middle(1), 0)
-    sum_a(1)
-    sum_c(2)
+    sum_c(0)
+    sum_d(2)
+    sum_d(1)
+    extra_e()
     sum_e(3)
-
-    def first(chunk, _):
-        first_grad(chunk)
-        return 0
-
-    lax.fori_loop(0, 2, first, 0)
-    sum_b(1)
-    sum_d(2)
-    lax.fori_loop(2, 4, first, 0)
-    g_ref[0] = g_ref[0].T
-    sum_a(0)
-    sum_c(1)
     sum_e(2)
-
-    def last(chunk, _):
-        first_back(chunk)
-        return 0
-
-    lax.fori_loop(0, 2, last, 0)
-    for side in range(2):
-        give(0, side).start()
-    sum_b(0)
-    sum_d(1)
-    lax.fori_loop(2, 4, last, 0)
-    for side in range(2):
-        give(1, side).start()
-    sum_c(0)
+    sum_d(0)
     sum_e(1)
-    extra_e()
-    sum_d(0)
     sum_e(0)
     for g in range(n_groups):
-        for side in range(2):
-            give(g, side).wait()
-    for g in range(n_groups):
-        each(n_cell, functools.partial(t1, g), sent)
-        each(n_cell, functools.partial(e1, g), sent)
-        each(n_cell, functools.partial(e2, g), sent)
-    each(n_cell, igc, sent)
+        t1_all(g).wait_send()
+        e1_all(g).wait_send()
+        e2_all(g).wait_send()
+    igc_all().wait_send()
     ecc().wait_send()
-    each(n_spot, ebc, sent)
+    ebc_all().wait_send()
     efc().wait_send()
-    each(n_cell, iac, sent)
+    iac_all().wait_send()
     for l in range(LAYERS):
         cc(l).wait_send()
-        each(n_spot, functools.partial(rc, l), sent)
-        each(n_spot, functools.partial(ac, l), sent)
+        rc_all(l).wait_send()
+        ac_all(l).wait_send()
         sc(l).wait_send()
+
+
+def hand_over(lg_ref, hg_ref, ig_ref, og_ref, sg_ref, lg_hbm, hg_hbm, ig_hbm, og_hbm, sg_hbm, sems):
+    copies = [
+        pltpu.make_async_copy(src, dst, sems.at[n])
+        for n, (src, dst) in enumerate(
+            ((lg_ref, lg_hbm), (hg_ref, hg_hbm), (ig_ref, ig_hbm), (og_ref, og_hbm))
+        )
+    ]
+    for side in range(2):
+        lanes = pl.ds(side * 128, 128)
+        copies.append(pltpu.make_async_copy(sg_ref.at[side], sg_hbm.at[:, lanes], sems.at[4 + side]))
+    for c in copies[::-1]:
+        c.start()
+    for c in copies:
+        c.wait()
 
 
 def local(n_cell, encodings, spacing, counts, cell_weights, density_head, decoder_in, decoder_out, color_grad):
@@ -552,7 +591,14 @@
     dma = pltpu.SemaphoreType.DMA
     V = pltpu.VMEM
     scratch = [
-        V((2, rows, 128), F32),
+        V((slots, rays), F32),
+        V((1, rays), jnp.int32),
+        V((LAYERS, D, D), F32),
+        V((1, D), F32),
+        V((D, D), F32),
+        V((COLORS, D), F32),
+        V((COLORS, rays), F32),
+        V((groups, GROUP, GROUP), F32),
         V((LAYERS - 1, 2, chunks, D, wide), BF16),
         V((LAYERS, chunks, D, wide), F32),
         V((chunks, D, wide), F32),
@@ -564,8 +610,6 @@
         V((3 * D, D), BF16),
         V((D, 3 * D), BF16),
         V((D, GROUP), F32),
-        V((8, D), F32),
-        V((GROUP, GROUP), F32),
         V((groups, SLOTS, GROUP), F32),
         V((groups, 8, SLOTS, GROUP), F32),
         V((GROUP, GROUP), F32),
@@ -585,46 +629,53 @@
         V((24, D), F32),
         V((8, 24, D), F32),
         V((48, D), F32),
-        V((n_cell, 32, D), F32),
         V((LAYERS, D, D), F32),
         V((LAYERS, 128, D), F32),
         V((LAYERS, 128, D), F32),
         V((LAYERS, 8, 16, D), F32),
-        V((LAYERS, D, D), F32),
-        dma((groups, 2)), dma((groups, 2)),
-        dma((groups, n_cell)), dma((groups, n_cell)),
-        dma((groups, n_cell)), dma((groups, n_cell)),
-        dma((groups, n_cell)), dma((groups, n_cell)),
-        dma((n_cell,)), dma((n_cell,)),
+        dma((groups, 2)), dma((6 + LAYERS,)),
+        dma((groups,)), dma((groups,)),
+        dma((groups,)), dma((groups,)),
+        dma((groups,)), dma((groups,)),
         dma((1,)), dma((1,)),
-        dma((8,)), dma((8,)),
         dma((1,)), dma((1,)),
-        dma((n_cell,)), dma((n_cell,)),
+        dma((1,)), dma((1,)),
+        dma((1,)), dma((1,)),
+        dma((1,)), dma((1,)),
         dma((LAYERS,)), dma((LAYERS,)),
-        dma((LAYERS, 8)), dma((LAYERS, 8)),
-        dma((LAYERS, 8)), dma((LAYERS, 8)),
+        dma((LAYERS,)), dma((LAYERS,)),
+        dma((LAYERS,)), dma((LAYERS,)),
         dma((LAYERS,)), dma((LAYERS,)),
     ]
+    outs = [V((LAYERS, D, D), F32), V((1, D), F32), V((n_cell, 32, D), F32), V((COLORS, D), F32), V((2, rows, 128), F32)]
+    parts = pl.pallas_call(
+        functools.partial(kernel, n_cell),
+        out_shape=outs,
+        in_specs=[anywhere] * 8,
+        out_specs=[vmem] * 5,
+        scratch_shapes=scratch,
+        compiler_params=pltpu.CompilerParams(
+            collective_id=0, has_side_effects=True, vmem_limit_bytes=56 << 20
+        ),
+    )(
+        encodings.reshape(rows, width), spacing.T, counts.T, cell_weights[0], density_head,
+        decoder_in, decoder_out.T, color_grad.T,
+    )
     layer, head, din, dout, sample = pl.pallas_call(
-        functools.partial(kernel, n_cell),
+        hand_over,
         out_shape=[
             jax.ShapeDtypeStruct((LAYERS, D, D), F32),
             jax.ShapeDtypeStruct((1, D), F32),
-            jax.ShapeDtypeStruct((D, D), F32),
-            jax.ShapeDtypeStruct((D, COLORS), F32),
+            jax.ShapeDtypeStruct((n_cell, 32, D), F32),
+            jax.ShapeDtypeStruct((COLORS, D), F32),
             jax.ShapeDtypeStruct((rows, D), F32),
         ],
-        in_specs=[anywhere] + [vmem] * 7,
-        out_specs=[vmem] * 4 + [anywhere],
-        scratch_shapes=scratch,
-        compiler_params=pltpu.CompilerParams(
-            collective_id=0, has_side_effects=True, vmem_limit_bytes=62 << 20
-        ),
-    )(
-        encodings.reshape(rows, width), spacing, counts, cell_weights[0], density_head,
-        decoder_in, decoder_out, color_grad,
-    )
-    return layer[None], head, din, dout, sample.reshape(rays, slots, width)
+        in_specs=[vmem] * 5,
+        out_specs=[anywhere] * 5,
+        scratch_shapes=[dma((6,))],
+        compiler_params=pltpu.CompilerParams(vmem_limit_bytes=1 << 20),
+    )(*(pltpu.with_memory_space_constraint(part, pltpu.VMEM) for part in parts))
+    return layer[None], head, din.reshape(D, D), dout.T, sample.reshape(rays, slots, width)
 
 
 def solution(mesh):

time: 97.3 us -> 66.7 us (0.69)
  local copies, waits for them, and re-layouts: 17.3 us -> 0 us
  Pallas kernels: 79 us -> 65.8 us
    unnamed x9 -> x0, local copies, waits for them, and re-layouts: 17.3 us -> none
    pallas_call x1 -> x2, Pallas kernels: 79 us -> 65.8 us  [the longest x1 63.3 us: local(): pl.pallas_call(functools.partial(kernel, n_cell), out_shape=outs, in_spec...]
where the time goes in v1:
time: 66.7 us; the launch traced here: 66.6 us
  Pallas kernels  65.8 us (99%)
  between operations  0.8 us (1%)
    pallas_call x1, Pallas kernels, local(): pl.pallas_call(functools.partial(kernel, n_cell), out_shape=outs, in_spec...  63.3 us
    pallas_call x1, Pallas kernels, local(): pl.pallas_call(hand_over, out_shape=[jax.ShapeDtypeStruct((LAYERS, D, D),...  2.5 us

profile of v1, /device:TPU:1, one launch (start us, length us, event | category | flops | bytes accessed | tf_op | source)
XLA Modules:
  0.0 66.6 jit_solution(15129246630867185008)
XLA Ops:
  0.6 63.3 %shard_map.119 = (f32[4,256,256]{2,1,0:T(8,128)S(1)}, f32[1,256]{1,0:T(1,128)S(1)}, f32[8,32,256]{2,1,0:T(8,128)S(1)}, f32[3,256]{1,0:T(4,128)S(1)}, f32[2,4096,128]{2,1,0:T(8,128)S(1)}) custom-call(f32[4096,256]{1,0:T(8,128)} %bitcast.10, f32[16,256]{1,0:T(8,128)} %bitcast.12, s32[1,256]{1,0:T(1,128)} %bitcast.15, f32[4,256,256]{2,1,0:T(8,128)} %bitcast.11, ...), custom_call_target="tpu_custom_call" | custom-call | tf_op jit(solution)/shard_map/pallas_call | solution.py:651
  63.9 2.5 %shard_map.120 = (f32[4,256,256]{2,1,0:T(8,128)}, f32[1,256]{1,0:T(1,128)}, f32[8,32,256]{2,1,0:T(8,128)}, f32[3,256]{1,0:T(4,128)}, f32[4096,256]{1,0:T(8,128)}) custom-call(f32[4,256,256]{2,1,0:T(8,128)S(1)} %get-tuple-element.15.lg_ref, f32[1,256]{1,0:T(1,128)S(1)} %get-tuple-element.16.hg_ref, f32[8,32,256]{2,1,0:T(8,128)S(1)} %get-tuple-element.17.ig_ref, ...), custom_call_target="tpu_custom_call" | custom-call | tf_op jit(solution)/shard_map/pallas_call | solution.py:664

commit v2 on v1

--- a/solution.py
+++ b/solution.py
@@ -70,10 +70,10 @@
     wt_ref, wb_ref, v_ref, dv_ref, dh_ref, headt_ref,
     z_ref, sm_ref, et_ref, hacc_ref,
     p_ref, pr_ref, t_ref, tr_ref, q_ref, qs_ref, px_ref, dpre_ref, ogs_ref,
-    igs_ref, igr_ref, ex_ref, exc_ref, eb_ref, ef_ref,
+    igs_ref, igr_ref, ex_ref, exc_ref, eb_ref, ef_ref, hx_ref, xs_ref,
     g_ref, cr_ref, half_ref, rr_ref,
     x_sem, in_sem, e1_send, e1_recv, t_send, t_recv, e2_send, e2_recv,
-    ig_send, ig_recv, ec_send, ec_recv, eb_send, eb_recv, ef_send, ef_recv, ia_send, ia_recv,
+    ig_send, ig_recv, ec_send, ec_recv, eb_send, eb_recv, ef_send, ef_recv, ia_send, ia_recv, hx_send, hx_recv,
     c_send, c_recv, r_send, r_recv, a_send, a_recv, s_send, s_recv,
 ):
     me = lax.axis_index("cell")
@@ -114,15 +114,21 @@
     def spot_peer(d):
         return {"rays": 2 * lax.rem(spot + d, n_spot) + core}
 
+    def ray_peer(d):
+        return {"rays": lax.rem(ray + d, 2 * n_spot)}
+
     barrier = pltpu.get_barrier_semaphore()
 
     def greet(d, _):
         pl.semaphore_signal(barrier, inc=1, device_id=cell_peer(d))
-        pl.semaphore_signal(barrier, inc=1, device_id=spot_peer(d))
         return 0
 
+    def greet_rays(d, _):
+        pl.semaphore_signal(barrier, inc=1, device_id=ray_peer(d))
+        return 0
+
     lax.fori_loop(1, n_cell, greet, 0)
-    pl.semaphore_signal(barrier, inc=1, device_id={"rays": sibling})
+    lax.fori_loop(1, 2 * n_spot, greet_rays, 0)
 
     def remote(src, dst, send, recv, device):
         return pltpu.make_async_remote_copy(
@@ -189,6 +195,13 @@
     def iac_all():
         blocks = igf_ref.at[pl.ds(0, n_cell - 1)]
         return remote(blocks, blocks, ia_send.at[0], ia_recv.at[0], cell_peer(1))
+
+    def hx(d):
+        return remote(hx_ref.at[ray], hx_ref.at[ray], hx_send.at[0], hx_recv.at[0], ray_peer(d))
+
+    def hx_all():
+        blocks = hx_ref.at[pl.ds(0, 2 * n_spot - 1)]
+        return remote(blocks, blocks, hx_send.at[0], hx_recv.at[0], ray_peer(1))
 
     def cc(l):
         other = pl.ds(pl.multiple_of((1 - core) * 128, 128), 128)
@@ -398,10 +411,16 @@
             dph_ref[chunk, :, columns] = nhi
             dpl_ref[chunk, :, columns] = nlo
 
+    def x_split(chunk):
+        g, half = chunk // 2, lax.rem(chunk, 2)
+        for q in range(8):
+            hi, lo = split(x_load(g, 8 * half + q))
+            xs_ref[0, chunk, q * GROUP:(q + 1) * GROUP, :] = hi
+            xs_ref[1, chunk, q * GROUP:(q + 1) * GROUP, :] = lo
+
     def first_grad(chunk):
-        g, half = chunk // 2, lax.rem(chunk, 2)
-        rows = jnp.concatenate([x_load(g, 8 * half + q) for q in range(8)], axis=0)
-        g_ref[0] += mm(left3(dph_ref[chunk], dpl_ref[chunk], 1), right3(*split(rows), 0), NN)
+        rows = right3(xs_ref[0, chunk], xs_ref[1, chunk], 0)
+        g_ref[0] += mm(left3(dph_ref[chunk], dpl_ref[chunk], 1), rows, NN)
 
     def first_back(chunk):
         g, half = chunk // 2, lax.rem(chunk, 2)
@@ -444,7 +463,6 @@
         for j in range(1, n_cell):
             total = total + igr_ref[j]
         ex_ref[0:40, :] = total
-        ex_ref[40:48, :] = jnp.broadcast_to(jnp.sum(hacc_ref[...].T, axis=0, keepdims=True), (8, D))
         ecc().start()
 
     def extra_b():
@@ -468,7 +486,17 @@
     def extra_e():
         iac_all().wait_recv()
         og_ref[...] = ef_ref[32:32 + COLORS, :]
-        hg_ref[...] = ef_ref[40:41, :]
+
+    def head_a():
+        hx_ref[ray] = jnp.broadcast_to(jnp.sum(hacc_ref[...].T, axis=0, keepdims=True), (8, D))
+        each(2 * n_spot, hx)
+
+    def head_b():
+        hx_all().wait_recv()
+        total = hx_ref[0]
+        for j in range(1, 2 * n_spot):
+            total = total + hx_ref[j]
+        hg_ref[...] = total[0:1, :]
 
     def wait_x(g):
         for side in range(2):
@@ -481,9 +509,11 @@
 
         lax.fori_loop(0, 2, body, 0)
 
-    def rest(first_chunk, step):
+    def rest(first_chunk, step, between=None):
         def body(chunk, _):
             step(chunk)
+            if between is not None:
+                pl.when(chunk == first_chunk)(between)
             return 0
 
         lax.fori_loop(first_chunk, first_chunk + 2, body, 0)
@@ -499,7 +529,7 @@
         forward_weights(l)
     wait_x(0)
     forward_loop(0)
-    pl.semaphore_wait(barrier, 2 * (n_cell - 1) + 1)
+    pl.semaphore_wait(barrier, n_cell - 1 + 2 * n_spot - 1)
     rays_forward(0)
     wait_x(1)
     forward_loop(1)
@@ -509,41 +539,45 @@
     backward_weights()
     g_ref[...] = jnp.zeros_like(g_ref)
     hacc_ref[...] = jnp.zeros_like(hacc_ref)
+    ex_ref[40:48, :] = jnp.zeros((8, D), F32)
+    rest(0, x_split)
+    rest(2, x_split)
+    decode(1)
+    decoder_grads()
     rays_backward(0)
     rest(0, top)
-    decode(1)
     rest(0, middle[2])
-    decoder_grads()
-    rest(0, middle[1])
     rays_backward(1)
-    rest(2, top)
+    extra_a()
+    rest(2, top, extra_b)
     sum_a(3)
-    extra_a()
-    rest(2, middle[2])
-    sum_b(3)
-    extra_b()
+    head_a()
+
+    rest(2, middle[2], lambda: sum_b(3))
     sum_a(2)
-    rest(2, middle[1])
-    sum_b(2)
+    rest(0, middle[1], lambda: sum_b(2))
+    rest(2, middle[1], extra_c)
     sum_a(1)
-    rest(0, first_grad)
-    sum_b(1)
+    extra_d()
+
+    def sums_b1_c3():
+        sum_b(1)
+        sum_c(3)
+
+    rest(0, first_grad, sums_b1_c3)
     rest(2, first_grad)
     g_ref[0] = g_ref[0].T
     sum_a(0)
-    sum_c(3)
-    extra_c()
-    rest(0, first_back)
-    sum_b(0)
+    rest(0, first_back, lambda: sum_b(0))
     sum_c(2)
-    extra_d()
     rest(2, first_back)
     sum_c(1)
     sum_d(3)
+    head_b()
     sum_c(0)
     sum_d(2)
+    extra_e()
     sum_d(1)
-    extra_e()
     sum_e(3)
     sum_e(2)
     sum_d(0)
@@ -558,6 +592,7 @@
     ebc_all().wait_send()
     efc().wait_send()
     iac_all().wait_send()
+    hx_all().wait_send()
     for l in range(LAYERS):
         cc(l).wait_send()
         rc_all(l).wait_send()
@@ -629,6 +664,8 @@
         V((24, D), F32),
         V((8, 24, D), F32),
         V((48, D), F32),
+        V((16, 8, D), F32),
+        V((2, chunks, wide, D), BF16),
         V((LAYERS, D, D), F32),
         V((LAYERS, 128, D), F32),
         V((LAYERS, 128, D), F32),
@@ -637,6 +674,7 @@
         dma((groups,)), dma((groups,)),
         dma((groups,)), dma((groups,)),
         dma((groups,)), dma((groups,)),
+        dma((1,)), dma((1,)),
         dma((1,)), dma((1,)),
         dma((1,)), dma((1,)),
         dma((1,)), dma((1,)),

time: 66.7 us -> 63.3 us (0.949)
  Pallas kernels: 65.8 us -> 62.4 us
    pallas_call x1, Pallas kernels: 63.3 us -> 59.9 us  [local(): pl.pallas_call(functools.partial(kernel, n_cell), out_shape=outs, in_spec...]
where the time goes in v2:
time: 63.3 us; the launch traced here: 63.2 us
  Pallas kernels  62.4 us (99%)
  between operations  0.8 us (1%)
    pallas_call x1, Pallas kernels, local(): pl.pallas_call(functools.partial(kernel, n_cell), out_shape=outs, in_spec...  59.9 us
    pallas_call x1, Pallas kernels, local(): pl.pallas_call(hand_over, out_shape=[jax.ShapeDtypeStruct((LAYERS, D, D),...  2.5 us

profile of v2, /device:TPU:1, one launch (start us, length us, event | category | flops | bytes accessed | tf_op | source)
XLA Modules:
  0.0 63.2 jit_solution(1512326480590057131)
XLA Ops:
  0.6 59.9 %shard_map.119 = (f32[4,256,256]{2,1,0:T(8,128)S(1)}, f32[1,256]{1,0:T(1,128)S(1)}, f32[8,32,256]{2,1,0:T(8,128)S(1)}, f32[3,256]{1,0:T(4,128)S(1)}, f32[2,4096,128]{2,1,0:T(8,128)S(1)}) custom-call(f32[4096,256]{1,0:T(8,128)} %bitcast.10, f32[16,256]{1,0:T(8,128)} %bitcast.12, s32[1,256]{1,0:T(1,128)} %bitcast.15, f32[4,256,256]{2,1,0:T(8,128)} %bitcast.11, ...), custom_call_target="tpu_custom_call" | custom-call | tf_op jit(solution)/shard_map/pallas_call | solution.py:689
  60.6 2.5 %shard_map.120 = (f32[4,256,256]{2,1,0:T(8,128)}, f32[1,256]{1,0:T(1,128)}, f32[8,32,256]{2,1,0:T(8,128)}, f32[3,256]{1,0:T(4,128)}, f32[4096,256]{1,0:T(8,128)}) custom-call(f32[4,256,256]{2,1,0:T(8,128)S(1)} %get-tuple-element.15.lg_ref, f32[1,256]{1,0:T(1,128)S(1)} %get-tuple-element.16.hg_ref, f32[8,32,256]{2,1,0:T(8,128)S(1)} %get-tuple-element.17.ig_ref, ...), custom_call_target="tpu_custom_call" | custom-call | tf_op jit(solution)/shard_map/pallas_call | solution.py:702

commit v3 on v2

--- a/solution.py
+++ b/solution.py
@@ -69,10 +69,10 @@
     h_ref, s_ref, f_ref, dph_ref, dpl_ref,
     wt_ref, wb_ref, v_ref, dv_ref, dh_ref, headt_ref,
     z_ref, sm_ref, et_ref, hacc_ref,
-    p_ref, pr_ref, t_ref, tr_ref, q_ref, qs_ref, px_ref, dpre_ref, ogs_ref,
+    p_ref, pr_ref, t_ref, tr_ref, q_ref, qs_ref, l_ref, lr_ref, px_ref, dpre_ref, ogs_ref,
     igs_ref, igr_ref, ex_ref, exc_ref, eb_ref, ef_ref, hx_ref, xs_ref,
     g_ref, cr_ref, half_ref, rr_ref,
-    x_sem, in_sem, e1_send, e1_recv, t_send, t_recv, e2_send, e2_recv,
+    x_sem, in_sem, e1_send, e1_recv, t_send, t_recv, e2_send, e2_recv, l_send, l_recv,
     ig_send, ig_recv, ec_send, ec_recv, eb_send, eb_recv, ef_send, ef_recv, ia_send, ia_recv, hx_send, hx_recv,
     c_send, c_recv, r_send, r_recv, a_send, a_recv, s_send, s_recv,
 ):
@@ -164,6 +164,13 @@
     def e2_all(g):
         blocks = q_ref.at[g, pl.ds(0, GROUP - owned), :]
         return remote(blocks, blocks, e2_send.at[g], e2_recv.at[g], cell_peer(1))
+
+    def l2(g, d):
+        return remote(l_ref.at[g], lr_ref.at[g, me], l_send.at[g], l_recv.at[g], cell_peer(d))
+
+    def l2_all(g):
+        blocks = lr_ref.at[g, pl.ds(0, n_cell - 1)]
+        return remote(blocks, blocks, l_send.at[g], l_recv.at[g], cell_peer(1))
 
     def igc(d):
         to = lax.rem(me + d, n_cell)
@@ -342,15 +349,20 @@
         for c in range(COLORS):
             ogs_ref[g, c:c + 1, :] = jnp.sum(act * colors[:, c:c + 1], axis=0, keepdims=True)
         grad = mm(right3(*split(dpre), 1), dh_ref[...], NT)
+        qs_ref[g] = grad
+        each(n_cell, functools.partial(e2, g))
+        q_ref[g, my_rows, :] = grad
         lanes = lax.broadcasted_iota(jnp.int32, (owned, GROUP), 1)
         later = jnp.zeros((owned, GROUP), F32)
         for j in range(1, n_cell):
             value = jnp.sum(parts[j] * grad, axis=1, keepdims=True)
             later = later + jnp.where(lanes < j, value, 0.0)
-        payload = jnp.concatenate([grad, later], axis=1)
-        qs_ref[g] = payload
-        each(n_cell, functools.partial(e2, g))
-        q_ref[g, my_rows, :] = payload
+        et_ref[...] = jnp.zeros_like(et_ref)
+        et_ref[my_rows, :] = later
+        tile = et_ref[...].T[0:8, :]
+        l_ref[g] = tile
+        lr_ref[g, me] = tile
+        each(n_cell, functools.partial(l2, g))
 
     def decoder_grads():
         px = right3(*split(px_ref[...].reshape(n_groups * owned, D)), 0)
@@ -367,13 +379,16 @@
 
     def rays_backward(g):
         e2_all(g).wait_recv()
-        gradt = q_ref[g, :, 0:D].T
-        latert = q_ref[g, :, D:D + GROUP].T[0:8, :]
-        picked = lax.broadcasted_iota(jnp.int32, (8, GROUP), 0) == me
-        later = jnp.sum(jnp.where(picked, latert, 0.0), axis=0, keepdims=True)
+        gradt = q_ref[g].T
         et_ref[...] = jnp.zeros_like(et_ref)
         for s in range(SLOTS):
             et_ref[s:s + 1, :] = jnp.sum(slot_of(f_ref, g, s) * gradt, axis=0, keepdims=True)
+        l2_all(g).wait_recv()
+        latert = lr_ref[g, 0]
+        for j in range(1, n_cell):
+            latert = latert + lr_ref[g, j]
+        picked = lax.broadcasted_iota(jnp.int32, (8, GROUP), 0) == me
+        later = jnp.sum(jnp.where(picked, latert, 0.0), axis=0, keepdims=True)
         c = et_ref[0:SLOTS, :]
         tau = sm_ref[g, 1]
         trans = jnp.exp(-(sm_ref[g, 5] + sm_ref[g, 2]))
@@ -388,17 +403,21 @@
 
     def head_step(chunk, l):
         g, half = chunk // 2, lax.rem(chunk, 2)
-        for q in range(8):
-            row = pl.ds(8 * half + q, 1)
-            weight, dz = sm_ref[g, 6, row, :], sm_ref[g, 7, row, :]
-            columns = pl.ds(q * GROUP, GROUP)
-            for part in range(2):
-                rows = pl.ds(part * 128, 128)
-                back = q_ref[g, :, part * GROUP:(part + 1) * GROUP] * weight + headt_ref[rows, :] * dz
-                hacc_ref[rows, :] += f_ref[chunk, rows, columns] * dz
+        for part in range(4):
+            rows = pl.ds(part * 64, 64)
+            gradt = q_ref[g, pl.ds((part % 2) * 64, 64), (part // 2) * GROUP:(part // 2 + 1) * GROUP]
+            head = headt_ref[rows, :]
+            acc = hacc_ref[rows, :]
+            for q in range(8):
+                row = pl.ds(8 * half + q, 1)
+                weight, dz = sm_ref[g, 6, row, :], sm_ref[g, 7, row, :]
+                columns = pl.ds(q * GROUP, GROUP)
+                acc = acc + f_ref[chunk, rows, columns] * dz
+                back = gradt * weight + head * dz
                 hi, lo = split(back * s_ref[LAYERS - 1, chunk, rows, columns])
                 dph_ref[chunk, rows, columns] = hi
                 dpl_ref[chunk, rows, columns] = lo
+            hacc_ref[rows, :] = acc
 
     def layer_step(chunk, l):
         hi, lo = dph_ref[chunk], dpl_ref[chunk]
@@ -587,6 +606,7 @@
         t1_all(g).wait_send()
         e1_all(g).wait_send()
         e2_all(g).wait_send()
+        l2_all(g).wait_send()
     igc_all().wait_send()
     ecc().wait_send()
     ebc_all().wait_send()
@@ -607,9 +627,11 @@
             ((lg_ref, lg_hbm), (hg_ref, hg_hbm), (ig_ref, ig_hbm), (og_ref, og_hbm))
         )
     ]
-    for side in range(2):
-        lanes = pl.ds(side * 128, 128)
-        copies.append(pltpu.make_async_copy(sg_ref.at[side], sg_hbm.at[:, lanes], sems.at[4 + side]))
+    pieces = 4
+    rows = sg_hbm.shape[0] // pieces
+    for n in range(2 * pieces):
+        part, lanes = pl.ds(n // 2 * rows, rows), pl.ds(n % 2 * 128, 128)
+        copies.append(pltpu.make_async_copy(sg_ref.at[n % 2, part, :], sg_hbm.at[part, lanes], sems.at[4 + n]))
     for c in copies[::-1]:
         c.start()
     for c in copies:
@@ -653,8 +675,10 @@
         V((groups, n_cell, owned, D), F32),
         V((groups, 8, GROUP), F32),
         V((groups, n_cell, 8, GROUP), F32),
-        V((groups, GROUP, D + GROUP), F32),
-        V((groups, owned, D + GROUP), F32),
+        V((groups, GROUP, D), F32),
+        V((groups, owned, D), F32),
+        V((groups, 8, GROUP), F32),
+        V((groups, n_cell, 8, GROUP), F32),
         V((groups, owned, D), F32),
         V((groups, owned, D), F32),
         V((groups, 8, D), F32),
@@ -671,6 +695,7 @@
         V((LAYERS, 128, D), F32),
         V((LAYERS, 8, 16, D), F32),
         dma((groups, 2)), dma((6 + LAYERS,)),
+        dma((groups,)), dma((groups,)),
         dma((groups,)), dma((groups,)),
         dma((groups,)), dma((groups,)),
         dma((groups,)), dma((groups,)),
@@ -710,7 +735,7 @@
         ],
         in_specs=[vmem] * 5,
         out_specs=[anywhere] * 5,
-        scratch_shapes=[dma((6,))],
+        scratch_shapes=[dma((12,))],
         compiler_params=pltpu.CompilerParams(vmem_limit_bytes=1 << 20),
     )(*(pltpu.with_memory_space_constraint(part, pltpu.VMEM) for part in parts))
     return layer[None], head, din.reshape(D, D), dout.T, sample.reshape(rays, slots, width)

time: 63.3 us -> 63 us (level)
  no operation moved by 1% of the time
where the time goes in v3:
time: 63 us; the launch traced here: 62.9 us
  Pallas kernels  62.1 us (99%)
  between operations  0.8 us (1%)
    pallas_call x1, Pallas kernels, local(): pl.pallas_call(functools.partial(kernel, n_cell), out_shape=outs, in_spec...  59.5 us
    pallas_call x1, Pallas kernels, local(): pl.pallas_call(hand_over, out_shape=[jax.ShapeDtypeStruct((LAYERS, D, D),...  2.56 us

profile of v3, /device:TPU:1, one launch (start us, length us, event | category | flops | bytes accessed | tf_op | source)
XLA Modules:
  0.0 62.9 jit_solution(10463924097987268783)
XLA Ops:
  0.6 59.5 %shard_map.119 = (f32[4,256,256]{2,1,0:T(8,128)S(1)}, f32[1,256]{1,0:T(1,128)S(1)}, f32[8,32,256]{2,1,0:T(8,128)S(1)}, f32[3,256]{1,0:T(4,128)S(1)}, f32[2,4096,128]{2,1,0:T(8,128)S(1)}) custom-call(f32[4096,256]{1,0:T(8,128)} %bitcast.10, f32[16,256]{1,0:T(8,128)} %bitcast.12, s32[1,256]{1,0:T(1,128)} %bitcast.15, f32[4,256,256]{2,1,0:T(8,128)} %bitcast.11, ...), custom_call_target="tpu_custom_call" | custom-call | tf_op jit(solution)/shard_map/pallas_call | solution.py:714
  60.1 2.6 %shard_map.120 = (f32[4,256,256]{2,1,0:T(8,128)}, f32[1,256]{1,0:T(1,128)}, f32[8,32,256]{2,1,0:T(8,128)}, f32[3,256]{1,0:T(4,128)}, f32[4096,256]{1,0:T(8,128)}) custom-call(f32[4,256,256]{2,1,0:T(8,128)S(1)} %get-tuple-element.15.lg_ref, f32[1,256]{1,0:T(1,128)S(1)} %get-tuple-element.16.hg_ref, f32[8,32,256]{2,1,0:T(8,128)S(1)} %get-tuple-element.17.ig_ref, ...), custom_call_target="tpu_custom_call" | custom-call | tf_op jit(solution)/shard_map/pallas_call | solution.py:727
